TPU v7x, 32 devices: a whole 2x2x4 slice. The times are simulated.
32 devices in a mesh: row: 2 (over y), col: 4 (over z), layer: 4 (over x, core).
Axes of the slice: x: 2, y: 2, z: 4, core: 2. Of those that a mesh axis runs over, the one named last changes fastest.
Arguments:
- eigvecs: float32 [16384, 8192], P('row', ('col', 'layer')), may hold values from -6 to 6
- first_vectors: float32 [16384, 128], P(('row', 'layer'), 'col'), may hold values from -0.375 to 0.375
- second_vectors: float32 [16384, 128], P(('row', 'layer'), 'col'), may hold values from -0.375 to 0.375
- first_factors: float32 [8192, 128], P(('row', 'layer'), 'col'), may hold values from -0.5 to 0.5
- second_factors: float32 [8192, 128], P(('row', 'layer'), 'col'), may hold values from -0.5 to 0.5
- panel_vectors: float32 [16384, 256], P(('row', 'layer')), may hold values from -0.125 to 0.125
- panel_factor: float32 [256, 256], replicated, may hold values from -0.375 to 0.375
Outputs:
- transformed: float32 [16384, 8192], P(('row', 'layer'), 'col')
All inputs are finite; a program needn't handle non-finite values.
Results may differ from a plain program's by a relative error of at most 0.000082.
Values sent between devices are 32-bit elements; how exact they have to be, the bound alone decides.
No kernel may reach another device: no remote copies, remote signals or barrier semaphores. Data moves between devices by JAX's collectives and lax.ppermute only.
A program may use at most 128 MiB of HBM per device.

v0:
```python
import jax
import jax.numpy as jnp
from jax import lax
from jax.sharding import PartitionSpec as P


def with_halo(array, sides, width):
    for axis, dim in sides:
        devices, length = (lax.axis_size(axis), array.shape[dim])
        up = [(i, (i + 1) % devices) for i in range(devices - 1)]
        down = [(j, i) for i, j in up]
        last = lax.slice_in_dim(array, length - width, length, axis=dim)
        first = lax.slice_in_dim(array, 0, width, axis=dim)
        before = lax.ppermute(last, axis, up)
        after = lax.ppermute(first, axis, down)
        array = jnp.concatenate([before, array, after], axis=dim)
    return array


def from_behind(value, axis, steps):
    count = lax.axis_size(axis)
    first, last = (max(0, -steps), min(count, count - steps))
    return lax.ppermute(value, axis, [(source, source + steps) for source in range(first, last)])


def apply_windows(data, vectors, factors):
    count = factors.shape[0] // 128
    width = data.shape[1]
    blocks = data.reshape(count, 256, width)
    vec_blocks = vectors.reshape(count, 256, 128)
    tri_blocks = jnp.triu(factors.reshape(count, 128, 128))
    proj = jnp.einsum("kri,krc->kic", vec_blocks, blocks, precision=lax.Precision.HIGHEST)
    scaled = jnp.einsum("kij,kjc->kic", tri_blocks, proj, precision=lax.Precision.HIGHEST)
    update = jnp.einsum("kri,kic->krc", vec_blocks, scaled, precision=lax.Precision.HIGHEST)
    return (blocks - update).reshape(count * 256, width)


def band_sweeps(data, vec_first, vec_second, fac_first, fac_second, extend, following):
    height = data.shape[0]
    width = data.shape[1]
    aligned = apply_windows(data, vec_first, fac_first)
    padded = extend(jnp.concatenate([aligned, vec_second], axis=1))
    next_factor = following(fac_second[:128])
    extended = jnp.concatenate([fac_second, next_factor], axis=0)
    offset = apply_windows(padded[:, :width], padded[:, width:], extended)
    return offset[128 : height + 128]


def band_tile(data, vec_first, vec_second, fac_first, fac_second):

    def extend(joined):
        return with_halo(joined, ((("row", "layer"), 0),), 128)

    def following(factor):
        return from_behind(factor, ("row", "layer"), -1)

    return band_sweeps(data, vec_first, vec_second, fac_first, fac_second, extend, following)


def to_tiles(data):
    return lax.all_to_all(data, "layer", split_axis=0, concat_axis=1, tiled=True)


def panel_tile(data, panel_vectors, upper):
    partial_value = jnp.dot(
        panel_vectors.T, data, precision=lax.Precision.HIGHEST, preferred_element_type=jnp.float32
    )
    projection = lax.psum(partial_value, ("row", "layer"))
    weights = jnp.dot(
        upper, projection, precision=lax.Precision.HIGHEST, preferred_element_type=jnp.float32
    )
    return data - jnp.dot(
        panel_vectors, weights, precision=lax.Precision.HIGHEST, preferred_element_type=jnp.float32
    )


def on_device(
    eigvecs,
    first_vectors,
    second_vectors,
    first_factors,
    second_factors,
    panel_vectors,
    panel_factor,
):
    upper = jnp.triu(panel_factor)
    reflectors = (
        lax.all_gather(first_vectors, "col", axis=1, tiled=True),
        lax.all_gather(second_vectors, "col", axis=1, tiled=True),
        lax.all_gather(first_factors, "col", axis=1, tiled=True),
        lax.all_gather(second_factors, "col", axis=1, tiled=True),
    )
    tiles = to_tiles(eigvecs)
    tiles = band_tile(tiles, reflectors[0], reflectors[1], reflectors[2], reflectors[3])
    return panel_tile(tiles, panel_vectors, upper)


def solution(mesh):
    in_specs = (
        P("row", ("col", "layer")),
        P(("row", "layer"), "col"),
        P(("row", "layer"), "col"),
        P(("row", "layer"), "col"),
        P(("row", "layer"), "col"),
        P(("row", "layer"), None),
        P(),
    )
    out_specs = P(("row", "layer"), "col")
    return jax.shard_map(
        on_device, mesh=mesh, in_specs=in_specs, out_specs=out_specs, check_vma=False
    )
```

profile of v0, /device:TPU:0, one launch (start us, length us, event | category | flops | bytes accessed | tf_op | source)
XLA Modules:
  0.0 561.3 jit_solution(13967101943740955004)
XLA Ops:
  6.5 7.1 %all-to-all-start = ((f32[4,2048,512]{2,1,0:T(8,128)}), f32[4,2048,512]{2,1,0:T(8,128)}, u32[]{:S(2)}, u32[]{:S(2)}) async-start(f32[4,2048,512]{2,1,0:T(8,128)} %bitcast.38), calls=%async_computation | async-start | bytes 33554432 | tf_op jit(solution)/shard_map/all_to_all | solution.py:61
  15.2 20.1 %all_gather.12 = f32[1024,128]{0,1:T(8,128)S(1)} all-gather(f32[1024,32]{0,1:T(8,128)S(1)} %copy-done.6), channel_id=1, replica_groups=mesh['row'=2,'col'=4,'layer'=4] {'col'}, dimensions={1}, use_global_device_ids=true | all-gather | bytes 655360 | tf_op jit(solution)/shard_map/all_gather | solution.py:90
  36.5 13.3 %all-gather.3.cloned.1.call-done = f32[2048,128]{0,1:T(8,128)} async-done(((f32[2048,32]{0,1:T(8,128)}), f32[2048,128]{0,1:T(8,128)}) %all-gather.3.cloned.1.call-update) | async-done | bytes 1048592 | tf_op jit(solution)/shard_map/all_gather | solution.py:88
  49.8 2.6 copy.41
  52.4 26.1 %all-gather.5.cloned.1.call-done = f32[2048,128]{0,1:T(8,128)} async-done(((f32[2048,32]{0,1:T(8,128)}), f32[2048,128]{0,1:T(8,128)}) %all-gather.5.cloned.1.call-update) | async-done | bytes 1048592 | tf_op jit(solution)/shard_map/all_gather | solution.py:89
  78.5 1.5 copy.43
  80.1 117.2 %all-to-all-done = f32[4,2048,512]{2,1,0:T(8,128)} async-done(((f32[4,2048,512]{2,1,0:T(8,128)}), f32[4,2048,512]{2,1,0:T(8,128)}, u32[]{:S(2)}, u32[]{:S(2)}) %all-to-all-start) | async-done | bytes 16777248 | tf_op jit(solution)/shard_map/all_to_all | solution.py:61
  197.3 20.9 %copy.39 = f32[2048,4,512]{2,1,0:T(4,128)} copy(f32[2048,4,512]{2,0,1:T(8,128)} %bitcast.1) | data formatting | bytes 33554432 | tf_op jit(solution)/shard_map/all_to_all | solution.py:61
  218.2 20.5 %reshape.28 = f32[8,256,2048]{2,1,0:T(8,128)} reshape(f32[2048,4,512]{2,1,0:T(4,128)} %copy.39) | data formatting | bytes 33554432 | tf_op jit(solution)/shard_map/reshape | solution.py:29
  238.8 14.5 %fusion.16 = f32[8,128,2048]{2,1,0:T(8,128)S(1)} fusion(f32[8,256,128]{2,1,0:T(8,128)} %bitcast.41, f32[8,256,2048]{2,1,0:T(8,128)} %reshape.28), kind=kOutput, calls=%fused_computation.29 | convolution fusion | flops 6442450944 | bytes 26214400 | tf_op jit(solution)/shard_map/kri,krc->kic/dot_general | solution.py:32
  253.3 9.6 %fusion.2 = f32[8,128,2048]{2,1,0:T(8,128)} fusion(f32[8,128,2048]{2,1,0:T(8,128)S(1)} %fusion.16, f32[8,128,128]{2,1,0:T(8,128)S(1)} %bitcast.44, pred[128,128]{1,0:T(8,128)(4,1)S(1)} %iota_compare_fusion.2), kind=kOutput, calls=%fused_computation.11 | convolution fusion | flops 3221356544 | bytes 17317888 | tf_op jit(solution)/shard_map/kij,kjc->kic/dot_general | solution.py:33
  262.9 22.4 %bitcast_subtract_fusion.1 = f32[8,256,2048]{2,1,0:T(8,128)} fusion(f32[8,256,2048]{2,1,0:T(8,128)} %reshape.28, f32[8,128,2048]{2,1,0:T(8,128)} %fusion.2, f32[8,256,128]{2,1,0:T(8,128)S(1)} %bitcast.42), kind=kOutput, calls=%fused_computation.2 | convolution fusion | flops 6446645248 | bytes 42991616 | tf_op jit(solution)/shard_map/kri,kic->krc/dot_general | solution.py:34
  285.4 3.1 pad_maximum_fusion.3
  288.5 2.3 collective-permute-start
  290.8 1.3 collective-permute-start.1
  292.1 18.3 %all_gather.15 = f32[1024,128]{0,1:T(8,128)} all-gather(f32[1024,32]{0,1:T(8,128)S(1)} %copy-done.7), channel_id=1, replica_groups=mesh['row'=2,'col'=4,'layer'=4] {'col'}, dimensions={1}, use_global_device_ids=true | all-gather | bytes 655360 | tf_op jit(solution)/shard_map/all_gather | solution.py:91
  310.3 2.0 copy.45
  313.2 1.3 collective-permute-start.2
  314.5 1.8 collective-permute-done.2
  316.4 1.9 pad_maximum_fusion.4
  318.3 19.1 %pad_maximum_fusion = f32[2304,2176]{1,0:T(8,128)} fusion(f32[128,2176]{1,0:T(8,128)} %collective-permute-done.1, f32[2048,128]{1,0:T(8,128)S(1)} %copy.43, f32[2048,2048]{1,0:T(8,128)} %bitcast.30, f32[128,2176]{1,0:T(8,128)} %collective-permute-done), kind=kLoop, calls=%fused_computation | loop fusion | flops 15040512 | bytes 40108032 | tf_op jit(solution)/shard_map/concatenate | solution.py:16
  337.4 15.5 %slice.24 = f32[2304,2048]{1,0:T(8,128)} slice(f32[2304,2176]{1,0:T(8,128)} %pad_maximum_fusion), slice={[0:2304], [0:2048]} | slice | bytes 37748736 | tf_op jit(solution)/shard_map/slice | solution.py:45
  353.9 14.0 %fusion.17 = f32[9,128,2048]{2,1,0:T(8,128)S(1)} fusion(f32[9,256,128]{2,1,0:T(8,128)S(1)} %bitcast.39, f32[9,256,2048]{2,1,0:T(8,128)} %bitcast.34), kind=kOutput, calls=%fused_computation.30 | convolution fusion | flops 7247757312 | bytes 29491200 | tf_op jit(solution)/shard_map/kri,krc->kic/dot_general | solution.py:32
  367.9 11.8 %fusion = f32[9,128,2048]{2,1,0:T(8,128)} fusion(f32[9,128,2048]{2,1,0:T(8,128)S(1)} %fusion.17, f32[9,128,128]{2,1,0:T(8,128)} %bitcast.43, pred[128,128]{1,0:T(8,128)(4,1)S(1)} %iota_compare_fusion.2), kind=kOutput, calls=%fused_computation.9 | convolution fusion | flops 3624026112 | bytes 19480576 | tf_op jit(solution)/shard_map/kij,kjc->kic/dot_general | solution.py:33
  379.7 25.0 %convolution_subtract_fusion = f32[9,256,2048]{2,1,0:T(8,128)} fusion(f32[9,256,2048]{2,1,0:T(8,128)} %bitcast.35, f32[9,256,128]{2,1,0:T(8,128)S(1)} %bitcast.40, f32[9,128,2048]{2,1,0:T(8,128)} %fusion), kind=kOutput, calls=%fused_computation.3 | convolution fusion | flops 7252475904 | bytes 48365568 | tf_op jit(solution)/shard_map/kri,kic->krc/dot_general | solution.py:34
  404.7 29.7 %convolution_bitcast_fusion = f32[256,2048]{0,1:T(8,128)} fusion(f32[2048,256]{1,0:T(8,128)S(1)} %copy-done, f32[2304,2048]{1,0:T(8,128)} %bitcast.36), kind=kOutput, calls=%fused_computation.4 | convolution fusion | flops 12884901888 | bytes 20971520 | tf_op jit(solution)/shard_map/dot_general | solution.py:65
  434.5 11.8 %slice.26 = f32[2048,2048]{1,0:T(8,128)} slice(f32[2304,2048]{1,0:T(8,128)} %bitcast.37), slice={[128:2176], [0:2048]} | slice | bytes 33554432
  446.3 18.2 %copy.52 = f32[2048,2048]{0,1:T(8,128)} copy(f32[2048,2048]{1,0:T(8,128)} %slice.26) | data formatting | bytes 33554432
  464.5 35.2 %all-reduce.2.cloned.1.call-done = f32[256,2048]{0,1:T(8,128)} async-done(((f32[256,2048]{0,1:T(8,128)}), f32[256,2048]{0,1:T(8,128)}) %all-reduce.2.cloned.1.call-update) | async-done | bytes 2097168 | tf_op jit(solution)/shard_map/psum | solution.py:68
  499.7 3.5 fusion.6
  503.3 33.4 %bitcast_subtract_fusion = f32[2048,2048]{0,1:T(8,128)} fusion(f32[2048,2048]{0,1:T(8,128)} %copy.52, f32[256,2048]{1,0:T(8,128)S(1)} %fusion.6, f32[2048,256]{1,0:T(8,128)S(1)} %copy-done), kind=kOutput, calls=%fused_computation.1 | convolution fusion | flops 12889096192 | bytes 37748736 | tf_op jit(solution)/shard_map/dot_general | solution.py:72
  536.7 17.6 %copy.48 = f32[2048,2048]{1,0:T(8,128)} copy(f32[2048,2048]{0,1:T(8,128)} %bitcast_subtract_fusion) | data formatting | bytes 33554432 | tf_op jit(solution)/shard_map/sub | solution.py:72
  (39 shorter events, 4.5 us)
Async XLA Ops:
  6.5 398.2 %copy-start = (f32[2048,256]{1,0:T(8,128)S(1)}, f32[2048,256]{1,0:T(8,128)}, u32[]{:S(2)}) copy-start(f32[2048,256]{1,0:T(8,128)} %param.12) | copy-start | bytes 6291460
  6.5 8.7 %copy-start.6 = (f32[1024,32]{0,1:T(8,128)S(1)}, f32[1024,32]{0,1:T(8,128)}, u32[]{:S(2)}) copy-start(f32[1024,32]{0,1:T(8,128)} %param.10) | copy-start | bytes 393220
  6.5 190.8 %all-to-all-start = ((f32[4,2048,512]{2,1,0:T(8,128)}), f32[4,2048,512]{2,1,0:T(8,128)}, u32[]{:S(2)}, u32[]{:S(2)}) async-start(f32[4,2048,512]{2,1,0:T(8,128)} %bitcast.38), calls=%async_computation | async-start | bytes 33554432 | tf_op jit(solution)/shard_map/all_to_all | solution.py:61
  13.7 36.1 %all-gather.3.cloned.1.call-start = ((), (), s32[]{:S(2)}) async-start(), calls=%async_computation.1 | async-start | bytes 1310720 | tf_op jit(solution)/shard_map/all_gather | solution.py:88
  14.4 64.1 %all-gather.5.cloned.1.call-start = ((), (), s32[]{:S(2)}) async-start(), calls=%async_computation.2 | async-start | bytes 1310720 | tf_op jit(solution)/shard_map/all_gather | solution.py:89
  15.1 484.6 %all-reduce.2.cloned.1.call-start = ((), (), s32[]{:S(2)}) async-start(), calls=%async_computation.3 | async-start | bytes 4194304 | tf_op jit(solution)/shard_map/psum | solution.py:68
  238.8 14.5 %copy-start.4 = (f32[1024,128]{1,0:T(8,128)S(1)}, f32[1024,128]{1,0:T(8,128)}, u32[]{:S(2)}) copy-start(f32[1024,128]{1,0:T(8,128)} %copy.51) | copy-start | bytes 1572868
  253.3 9.6 %copy-start.3 = (f32[2048,128]{1,0:T(8,128)S(1)}, f32[2048,128]{1,0:T(8,128)}, u32[]{:S(2)}) copy-start(f32[2048,128]{1,0:T(8,128)} %copy.41) | copy-start | bytes 3145732
  285.4 6.7 %copy-start.7 = (f32[1024,32]{0,1:T(8,128)S(1)}, f32[1024,32]{0,1:T(8,128)}, u32[]{:S(2)}) copy-start(f32[1024,32]{0,1:T(8,128)} %param.11) | copy-start | bytes 393220
  288.5 29.8 %collective-permute-start = (f32[128,2176]{1,0:T(8,128)}, f32[128,2176]{1,0:T(8,128)}, u32[]{:S(2)}, u32[]{:S(2)}) collective-permute-start(f32[128,2176]{1,0:T(8,128)} %get-tuple-element.5), channel_id=1, source_target_pairs={{0,1},{1,2},{2,3},{3,16},{16,17},{17,18},{18,19},{4,5},{5,6},{6,7}... | collective-permute-start | bytes 3342344 | tf_op jit(solution)/shard_map/ppermute | solution.py:14
  290.8 27.5 %collective-permute-start.1 = (f32[128,2176]{1,0:T(8,128)}, f32[128,2176]{1,0:T(8,128)}, u32[]{:S(2)}, u32[]{:S(2)}) collective-permute-start(f32[128,2176]{1,0:T(8,128)} %get-tuple-element.6), channel_id=1, source_target_pairs={{1,0},{2,1},{3,2},{16,3},{17,16},{18,17},{19,18},{5,4},{6,5},{7,6}... | collective-permute-start | bytes 3342344 | tf_op jit(solution)/shard_map/ppermute | solution.py:15
  313.2 3.1 collective-permute-start.2
  318.3 34.6 %slice-start = ((s8[16777216]{0:T(1024)(128)(4,1)}), s8[4194304]{0:T(1024)(128)(4,1)S(1)}, s32[]{:S(2)}) async-start(s8[16777216]{0:T(1024)(128)(4,1)} %bitcast.31), calls=%async_computation.4 | async-start | bytes 8388608
  318.3 34.6 %slice-start.1 = ((s8[16777216]{0:T(1024)(128)(4,1)}), s8[4194304]{0:T(1024)(128)(4,1)S(1)}, s32[]{:S(2)}) async-start(s8[16777216]{0:T(1024)(128)(4,1)} %bitcast.31), calls=%async_computation.5 | async-start | bytes 8388608
  318.3 34.6 %slice-start.2 = ((s8[16777216]{0:T(1024)(128)(4,1)}), s8[4194304]{0:T(1024)(128)(4,1)S(1)}, s32[]{:S(2)}) async-start(s8[16777216]{0:T(1024)(128)(4,1)} %bitcast.31), calls=%async_computation.6 | async-start | bytes 8388608
  337.4 15.5 %slice-start.3 = ((s8[16777216]{0:T(1024)(128)(4,1)}), s8[4194304]{0:T(1024)(128)(4,1)S(1)}, s32[]{:S(2)}) async-start(s8[16777216]{0:T(1024)(128)(4,1)} %bitcast.31), calls=%async_computation.7 | async-start | bytes 8388608
  353.9 14.0 %copy-start.1 = (f32[2304,128]{1,0:T(8,128)}, f32[2304,128]{1,0:T(8,128)S(1)}, u32[]{:S(2)}) copy-start(f32[2304,128]{1,0:T(8,128)S(1)} %pad_maximum_fusion.1) | copy-start | bytes 3538948
  367.9 11.9 %copy-start.2 = (f32[2304,128]{1,0:T(8,128)S(1)}, f32[2304,128]{1,0:T(8,128)}, u32[]{:S(2)}) copy-start(f32[2304,128]{1,0:T(8,128)} %copy-done.1) | copy-start | bytes 3538948
  446.3 53.5 %copy-start.5 = (f32[256,256]{1,0:T(8,128)S(1)}, f32[256,256]{1,0:T(8,128)}, u32[]{:S(2)}) copy-start(f32[256,256]{1,0:T(8,128)} %param.13) | copy-start | bytes 786436
Sparse Core Ops, SparseCore 0:
  16.0 33.7 all-gather.2
  51.4 27.1 all-gather.4
  434.6 65.1 all-reduce.1
where the time goes:
time: 572 us; the launch traced here: 561 us
  waiting for transfers between devices  195 us (34%)
  matrix products  164 us (29%)
  local copies, waits for them, and re-layouts  113 us (20%)
  blocking collectives  38.4 us (7%)
  other arithmetic  25.2 us (4%)
  between operations  13.7 us (2%)
  starting transfers between devices  12.1 us (2%)
    all_to_all x1, waiting for transfers between devices, to_tiles(): lax.all_to_all(data, 'layer', split_axis=0, concat_axis=1, tiled=True)  117 us
    dot_general x2, matrix products, apply_windows(): jnp.einsum('kri,kic->krc', vec_blocks, scaled, precision=lax.Precision.HI...  47.4 us
    psum x1, waiting for transfers between devices, panel_tile(): projection = lax.psum(partial_value, ('row', 'layer'))  35.2 us
    dot_general x1, matrix products, panel_tile(): jnp.dot(panel_vectors, weights, precision=lax.Precision.HIGHEST, preferre...  33.4 us
    unnamed x26, local copies, waits for them, and re-layouts  30.1 us
    dot_general x1, matrix products, panel_tile(): jnp.dot(panel_vectors.T, data, precision=lax.Precision.HIGHEST, preferred...  29.7 us
    dot_general x2, matrix products, apply_windows(): jnp.einsum('kri,krc->kic', vec_blocks, blocks, precision=lax.Precision.HI...  28.5 us
    all_gather x1, waiting for transfers between devices, on_device(): lax.all_gather(second_vectors, 'col', axis=1, tiled=True)  26.1 us
  transfers between devices with their start and end apart: 7, of which 5 were waited for; matrix products, arithmetic and copies ran while one was open for 7% of the time, Pallas kernels for 0%

commit v1 on v0

--- a/solution.py
+++ b/solution.py
@@ -65,7 +65,7 @@
     partial_value = jnp.dot(
         panel_vectors.T, data, precision=lax.Precision.HIGHEST, preferred_element_type=jnp.float32
     )
-    projection = lax.psum(partial_value, ("row", "layer"))
+    projection = lax.psum(lax.psum(partial_value, "layer"), "row")
     weights = jnp.dot(
         upper, projection, precision=lax.Precision.HIGHEST, preferred_element_type=jnp.float32
     )

time: 572 us -> 627 us (1.096)
  waiting for transfers between devices: 195 us -> 250 us
    psum x1 -> x2, waiting for transfers between devices: 35.2 us -> 90 us  [panel_tile(): projection = lax.psum(lax.psum(partial_value, 'layer'), 'row')]
  transfers between devices with their start and end apart: 7 -> 8, of which waited for: 5 -> 6; matrix products, arithmetic and copies ran while one was open for 7% -> 7% of each run, Pallas kernels for 0% -> 0%
where the time goes in v1:
time: 627 us; the launch traced here: 616 us
  waiting for transfers between devices  250 us (40%)
  matrix products  164 us (26%)
  local copies, waits for them, and re-layouts  113 us (18%)
  blocking collectives  38.4 us (6%)
  other arithmetic  25.2 us (4%)
  between operations  13.8 us (2%)
  starting transfers between devices  12.1 us (2%)
    all_to_all x1, waiting for transfers between devices, to_tiles(): lax.all_to_all(data, 'layer', split_axis=0, concat_axis=1, tiled=True)  117 us
    psum x2, waiting for transfers between devices, panel_tile(): projection = lax.psum(lax.psum(partial_value, 'layer'), 'row')  90 us
    dot_general x2, matrix products, apply_windows(): jnp.einsum('kri,kic->krc', vec_blocks, scaled, precision=lax.Precision.HI...  47.4 us
    dot_general x1, matrix products, panel_tile(): jnp.dot(panel_vectors, weights, precision=lax.Precision.HIGHEST, preferre...  33.4 us
    unnamed x26, local copies, waits for them, and re-layouts  30.1 us
    dot_general x1, matrix products, panel_tile(): jnp.dot(panel_vectors.T, data, precision=lax.Precision.HIGHEST, preferred...  29.7 us
    dot_general x2, matrix products, apply_windows(): jnp.einsum('kri,krc->kic', vec_blocks, blocks, precision=lax.Precision.HI...  28.5 us
    all_gather x1, waiting for transfers between devices, on_device(): lax.all_gather(second_vectors, 'col', axis=1, tiled=True)  26.1 us
  transfers between devices with their start and end apart: 8, of which 6 were waited for; matrix products, arithmetic and copies ran while one was open for 7% of the time, Pallas kernels for 0%

profile of v1, /device:TPU:0, one launch (start us, length us, event | category | flops | bytes accessed | tf_op | source)
XLA Modules:
  0.0 616.1 jit_solution(15783956645319989436)
XLA Ops:
  6.5 7.1 %all-to-all-start = ((f32[4,2048,512]{2,1,0:T(8,128)}), f32[4,2048,512]{2,1,0:T(8,128)}, u32[]{:S(2)}, u32[]{:S(2)}) async-start(f32[4,2048,512]{2,1,0:T(8,128)} %bitcast.38), calls=%async_computation | async-start | bytes 33554432 | tf_op jit(solution)/shard_map/all_to_all | solution.py:61
  15.2 20.1 %all_gather.12 = f32[1024,128]{0,1:T(8,128)S(1)} all-gather(f32[1024,32]{0,1:T(8,128)S(1)} %copy-done.6), channel_id=1, replica_groups=mesh['row'=2,'col'=4,'layer'=4] {'col'}, dimensions={1}, use_global_device_ids=true | all-gather | bytes 655360 | tf_op jit(solution)/shard_map/all_gather | solution.py:90
  36.5 13.3 %all-gather.3.cloned.1.call-done = f32[2048,128]{0,1:T(8,128)} async-done(((f32[2048,32]{0,1:T(8,128)}), f32[2048,128]{0,1:T(8,128)}) %all-gather.3.cloned.1.call-update) | async-done | bytes 1048592 | tf_op jit(solution)/shard_map/all_gather | solution.py:88
  49.8 2.6 copy.41
  52.4 26.1 %all-gather.5.cloned.1.call-done = f32[2048,128]{0,1:T(8,128)} async-done(((f32[2048,32]{0,1:T(8,128)}), f32[2048,128]{0,1:T(8,128)}) %all-gather.5.cloned.1.call-update) | async-done | bytes 1048592 | tf_op jit(solution)/shard_map/all_gather | solution.py:89
  78.5 1.5 copy.43
  80.1 117.2 %all-to-all-done = f32[4,2048,512]{2,1,0:T(8,128)} async-done(((f32[4,2048,512]{2,1,0:T(8,128)}), f32[4,2048,512]{2,1,0:T(8,128)}, u32[]{:S(2)}, u32[]{:S(2)}) %all-to-all-start) | async-done | bytes 16777248 | tf_op jit(solution)/shard_map/all_to_all | solution.py:61
  197.3 20.9 %copy.39 = f32[2048,4,512]{2,1,0:T(4,128)} copy(f32[2048,4,512]{2,0,1:T(8,128)} %bitcast.1) | data formatting | bytes 33554432 | tf_op jit(solution)/shard_map/all_to_all | solution.py:61
  218.2 20.5 %reshape.28 = f32[8,256,2048]{2,1,0:T(8,128)} reshape(f32[2048,4,512]{2,1,0:T(4,128)} %copy.39) | data formatting | bytes 33554432 | tf_op jit(solution)/shard_map/reshape | solution.py:29
  238.8 14.5 %fusion.16 = f32[8,128,2048]{2,1,0:T(8,128)S(1)} fusion(f32[8,256,128]{2,1,0:T(8,128)} %bitcast.41, f32[8,256,2048]{2,1,0:T(8,128)} %reshape.28), kind=kOutput, calls=%fused_computation.29 | convolution fusion | flops 6442450944 | bytes 26214400 | tf_op jit(solution)/shard_map/kri,krc->kic/dot_general | solution.py:32
  253.3 9.6 %fusion.2 = f32[8,128,2048]{2,1,0:T(8,128)} fusion(f32[8,128,2048]{2,1,0:T(8,128)S(1)} %fusion.16, f32[8,128,128]{2,1,0:T(8,128)S(1)} %bitcast.44, pred[128,128]{1,0:T(8,128)(4,1)S(1)} %iota_compare_fusion.2), kind=kOutput, calls=%fused_computation.11 | convolution fusion | flops 3221356544 | bytes 17317888 | tf_op jit(solution)/shard_map/kij,kjc->kic/dot_general | solution.py:33
  262.9 22.4 %bitcast_subtract_fusion.1 = f32[8,256,2048]{2,1,0:T(8,128)} fusion(f32[8,256,2048]{2,1,0:T(8,128)} %reshape.28, f32[8,128,2048]{2,1,0:T(8,128)} %fusion.2, f32[8,256,128]{2,1,0:T(8,128)S(1)} %bitcast.42), kind=kOutput, calls=%fused_computation.2 | convolution fusion | flops 6446645248 | bytes 42991616 | tf_op jit(solution)/shard_map/kri,kic->krc/dot_general | solution.py:34
  285.4 3.1 pad_maximum_fusion.3
  288.5 2.3 collective-permute-start
  290.8 1.3 collective-permute-start.1
  292.1 18.3 %all_gather.15 = f32[1024,128]{0,1:T(8,128)} all-gather(f32[1024,32]{0,1:T(8,128)S(1)} %copy-done.7), channel_id=1, replica_groups=mesh['row'=2,'col'=4,'layer'=4] {'col'}, dimensions={1}, use_global_device_ids=true | all-gather | bytes 655360 | tf_op jit(solution)/shard_map/all_gather | solution.py:91
  310.3 2.0 copy.45
  314.5 1.8 collective-permute-done.2
  316.4 1.9 pad_maximum_fusion.4
  318.3 19.1 %pad_maximum_fusion = f32[2304,2176]{1,0:T(8,128)} fusion(f32[128,2176]{1,0:T(8,128)} %collective-permute-done.1, f32[2048,128]{1,0:T(8,128)S(1)} %copy.43, f32[2048,2048]{1,0:T(8,128)} %bitcast.30, f32[128,2176]{1,0:T(8,128)} %collective-permute-done), kind=kLoop, calls=%fused_computation | loop fusion | flops 15040512 | bytes 40108032 | tf_op jit(solution)/shard_map/concatenate | solution.py:16
  337.4 15.5 %slice.24 = f32[2304,2048]{1,0:T(8,128)} slice(f32[2304,2176]{1,0:T(8,128)} %pad_maximum_fusion), slice={[0:2304], [0:2048]} | slice | bytes 37748736 | tf_op jit(solution)/shard_map/slice | solution.py:45
  353.9 14.0 %fusion.17 = f32[9,128,2048]{2,1,0:T(8,128)S(1)} fusion(f32[9,256,128]{2,1,0:T(8,128)S(1)} %bitcast.39, f32[9,256,2048]{2,1,0:T(8,128)} %bitcast.34), kind=kOutput, calls=%fused_computation.30 | convolution fusion | flops 7247757312 | bytes 29491200 | tf_op jit(solution)/shard_map/kri,krc->kic/dot_general | solution.py:32
  367.9 11.8 %fusion = f32[9,128,2048]{2,1,0:T(8,128)} fusion(f32[9,128,2048]{2,1,0:T(8,128)S(1)} %fusion.17, f32[9,128,128]{2,1,0:T(8,128)} %bitcast.43, pred[128,128]{1,0:T(8,128)(4,1)S(1)} %iota_compare_fusion.2), kind=kOutput, calls=%fused_computation.9 | convolution fusion | flops 3624026112 | bytes 19480576 | tf_op jit(solution)/shard_map/kij,kjc->kic/dot_general | solution.py:33
  379.7 25.0 %convolution_subtract_fusion = f32[9,256,2048]{2,1,0:T(8,128)} fusion(f32[9,256,2048]{2,1,0:T(8,128)} %bitcast.35, f32[9,256,128]{2,1,0:T(8,128)S(1)} %bitcast.40, f32[9,128,2048]{2,1,0:T(8,128)} %fusion), kind=kOutput, calls=%fused_computation.3 | convolution fusion | flops 7252475904 | bytes 48365568 | tf_op jit(solution)/shard_map/kri,kic->krc/dot_general | solution.py:34
  404.7 29.7 %convolution_bitcast_fusion = f32[256,2048]{0,1:T(8,128)} fusion(f32[2048,256]{1,0:T(8,128)S(1)} %copy-done, f32[2304,2048]{1,0:T(8,128)} %bitcast.36), kind=kOutput, calls=%fused_computation.4 | convolution fusion | flops 12884901888 | bytes 20971520 | tf_op jit(solution)/shard_map/dot_general | solution.py:65
  434.5 54.8 %all-reduce.3.cloned.1.call-done = f32[256,2048]{0,1:T(8,128)} async-done(((f32[256,2048]{0,1:T(8,128)}), f32[256,2048]{0,1:T(8,128)}) %all-reduce.3.cloned.1.call-update) | async-done | bytes 2097168 | tf_op jit(solution)/shard_map/psum | solution.py:68
  489.4 12.2 %slice.26 = f32[2048,2048]{1,0:T(8,128)} slice(f32[2304,2048]{1,0:T(8,128)} %bitcast.37), slice={[128:2176], [0:2048]} | slice | bytes 33554432
  501.6 17.8 %copy.52 = f32[2048,2048]{0,1:T(8,128)} copy(f32[2048,2048]{1,0:T(8,128)} %slice.26) | data formatting | bytes 33554432
  519.4 35.1 %all-reduce.5.cloned.1.call-done = f32[256,2048]{0,1:T(8,128)} async-done(((f32[256,2048]{0,1:T(8,128)}), f32[256,2048]{0,1:T(8,128)}) %all-reduce.5.cloned.1.call-update) | async-done | bytes 2097168 | tf_op jit(solution)/shard_map/psum | solution.py:68
  554.6 3.5 fusion.6
  558.1 33.4 %bitcast_subtract_fusion = f32[2048,2048]{0,1:T(8,128)} fusion(f32[2048,2048]{0,1:T(8,128)} %copy.52, f32[256,2048]{1,0:T(8,128)S(1)} %fusion.6, f32[2048,256]{1,0:T(8,128)S(1)} %copy-done), kind=kOutput, calls=%fused_computation.1 | convolution fusion | flops 12889096192 | bytes 37748736 | tf_op jit(solution)/shard_map/dot_general | solution.py:72
  591.5 17.6 %copy.48 = f32[2048,2048]{1,0:T(8,128)} copy(f32[2048,2048]{0,1:T(8,128)} %bitcast_subtract_fusion) | data formatting | bytes 33554432 | tf_op jit(solution)/shard_map/sub | solution.py:72
  (42 shorter events, 5.8 us)
Async XLA Ops:
  6.5 398.2 %copy-start = (f32[2048,256]{1,0:T(8,128)S(1)}, f32[2048,256]{1,0:T(8,128)}, u32[]{:S(2)}) copy-start(f32[2048,256]{1,0:T(8,128)} %param.12) | copy-start | bytes 6291460
  6.5 8.7 %copy-start.6 = (f32[1024,32]{0,1:T(8,128)S(1)}, f32[1024,32]{0,1:T(8,128)}, u32[]{:S(2)}) copy-start(f32[1024,32]{0,1:T(8,128)} %param.10) | copy-start | bytes 393220
  6.5 190.8 %all-to-all-start = ((f32[4,2048,512]{2,1,0:T(8,128)}), f32[4,2048,512]{2,1,0:T(8,128)}, u32[]{:S(2)}, u32[]{:S(2)}) async-start(f32[4,2048,512]{2,1,0:T(8,128)} %bitcast.38), calls=%async_computation | async-start | bytes 33554432 | tf_op jit(solution)/shard_map/all_to_all | solution.py:61
  13.7 36.1 %all-gather.3.cloned.1.call-start = ((), (), s32[]{:S(2)}) async-start(), calls=%async_computation.1 | async-start | bytes 1310720 | tf_op jit(solution)/shard_map/all_gather | solution.py:88
  14.4 64.1 %all-gather.5.cloned.1.call-start = ((), (), s32[]{:S(2)}) async-start(), calls=%async_computation.2 | async-start | bytes 1310720 | tf_op jit(solution)/shard_map/all_gather | solution.py:89
  15.1 474.2 %all-reduce.3.cloned.1.call-start = ((), (), s32[]{:S(2)}) async-start(), calls=%async_computation.3 | async-start | bytes 4194304 | tf_op jit(solution)/shard_map/psum | solution.py:68
  238.8 14.5 %copy-start.4 = (f32[1024,128]{1,0:T(8,128)S(1)}, f32[1024,128]{1,0:T(8,128)}, u32[]{:S(2)}) copy-start(f32[1024,128]{1,0:T(8,128)} %copy.51) | copy-start | bytes 1572868
  253.3 9.6 %copy-start.3 = (f32[2048,128]{1,0:T(8,128)S(1)}, f32[2048,128]{1,0:T(8,128)}, u32[]{:S(2)}) copy-start(f32[2048,128]{1,0:T(8,128)} %copy.41) | copy-start | bytes 3145732
  285.4 6.7 %copy-start.7 = (f32[1024,32]{0,1:T(8,128)S(1)}, f32[1024,32]{0,1:T(8,128)}, u32[]{:S(2)}) copy-start(f32[1024,32]{0,1:T(8,128)} %param.11) | copy-start | bytes 393220
  288.5 29.8 %collective-permute-start = (f32[128,2176]{1,0:T(8,128)}, f32[128,2176]{1,0:T(8,128)}, u32[]{:S(2)}, u32[]{:S(2)}) collective-permute-start(f32[128,2176]{1,0:T(8,128)} %get-tuple-element.5), channel_id=1, source_target_pairs={{0,1},{1,2},{2,3},{3,16},{16,17},{17,18},{18,19},{4,5},{5,6},{6,7}... | collective-permute-start | bytes 3342344 | tf_op jit(solution)/shard_map/ppermute | solution.py:14
  290.8 27.5 %collective-permute-start.1 = (f32[128,2176]{1,0:T(8,128)}, f32[128,2176]{1,0:T(8,128)}, u32[]{:S(2)}, u32[]{:S(2)}) collective-permute-start(f32[128,2176]{1,0:T(8,128)} %get-tuple-element.6), channel_id=1, source_target_pairs={{1,0},{2,1},{3,2},{16,3},{17,16},{18,17},{19,18},{5,4},{6,5},{7,6}... | collective-permute-start | bytes 3342344 | tf_op jit(solution)/shard_map/ppermute | solution.py:15
  313.2 3.1 collective-permute-start.2
  318.3 34.6 %slice-start = ((s8[16777216]{0:T(1024)(128)(4,1)}), s8[4194304]{0:T(1024)(128)(4,1)S(1)}, s32[]{:S(2)}) async-start(s8[16777216]{0:T(1024)(128)(4,1)} %bitcast.31), calls=%async_computation.5 | async-start | bytes 8388608
  318.3 34.6 %slice-start.1 = ((s8[16777216]{0:T(1024)(128)(4,1)}), s8[4194304]{0:T(1024)(128)(4,1)S(1)}, s32[]{:S(2)}) async-start(s8[16777216]{0:T(1024)(128)(4,1)} %bitcast.31), calls=%async_computation.6 | async-start | bytes 8388608
  318.3 34.6 %slice-start.2 = ((s8[16777216]{0:T(1024)(128)(4,1)}), s8[4194304]{0:T(1024)(128)(4,1)S(1)}, s32[]{:S(2)}) async-start(s8[16777216]{0:T(1024)(128)(4,1)} %bitcast.31), calls=%async_computation.7 | async-start | bytes 8388608
  337.4 15.5 %slice-start.3 = ((s8[16777216]{0:T(1024)(128)(4,1)}), s8[4194304]{0:T(1024)(128)(4,1)S(1)}, s32[]{:S(2)}) async-start(s8[16777216]{0:T(1024)(128)(4,1)} %bitcast.31), calls=%async_computation.8 | async-start | bytes 8388608
  353.9 14.0 %copy-start.1 = (f32[2304,128]{1,0:T(8,128)}, f32[2304,128]{1,0:T(8,128)S(1)}, u32[]{:S(2)}) copy-start(f32[2304,128]{1,0:T(8,128)S(1)} %pad_maximum_fusion.1) | copy-start | bytes 3538948
  367.9 11.9 %copy-start.2 = (f32[2304,128]{1,0:T(8,128)S(1)}, f32[2304,128]{1,0:T(8,128)}, u32[]{:S(2)}) copy-start(f32[2304,128]{1,0:T(8,128)} %copy-done.1) | copy-start | bytes 3538948
  434.4 120.1 %all-reduce.5.cloned.1.call-start = ((), (), s32[]{:S(2)}) async-start(), calls=%async_computation.4 | async-start | bytes 4194304 | tf_op jit(solution)/shard_map/psum | solution.py:68
  501.6 52.9 %copy-start.5 = (f32[256,256]{1,0:T(8,128)S(1)}, f32[256,256]{1,0:T(8,128)}, u32[]{:S(2)}) copy-start(f32[256,256]{1,0:T(8,128)} %param.13) | copy-start | bytes 786436
Sparse Core Ops, SparseCore 0:
  16.0 33.7 all-gather.2
  51.4 27.1 all-gather.4
  434.6 54.7 all-reduce.2
  491.5 63.0 all-reduce.4
